TPU v7x, 128 devices: a whole 4x4x4 slice. The times are simulated.
128 devices in a mesh: occ: 8 (over y, core), vir: 16 (over x, z).
Axes of the slice: x: 4, y: 4, z: 4, core: 2. Of those that a mesh axis runs over, the one named last changes fastest.
Arguments:
- amplitudes: bfloat16 [4096, 49152], P('occ', 'vir'), may hold values from -6 to 6
- integral_tiles: bfloat16 [16, 256, 128, 128], P('vir', 'occ'), may hold values from -0.0625 to 0.0625
- tile_cd: int32 [16, 256], replicated, may hold values from 0 to 23, as said below
- tile_ab: int32 [16, 256], replicated, may hold values from 0 to 63, as said below
- slot_tile: int32 [64], replicated, may hold values from 0 to 63, as said below
- residual_in: float32 [4096, 8192], P('occ', 'vir'), may hold values from -6 to 6
- occ_level: float32 [4096], P('occ'), may hold values from -3 to -1
- vir_level: float32 [8192], P('vir'), may hold values from 0.5 to 3
Outputs:
- update: float32 [4096, 8192], P('occ', 'vir')
Inputs may be any that keep to these rules, and one draw needn't show every extreme that they name: `tile_cd`: within a group no pair of contracted tile and slab tile repeats. `tile_ab`: for every group and every index w of vir, the group's tiles name slab tiles held in exactly 2 of the slots w * 4 to (w + 1) * 4 - 1. `slot_tile`: A permutation of the slab tiles.
All inputs are finite; a program needn't handle non-finite values.
Results may differ from a plain program's by a relative error of at most 0.0003.
Values may be sent and summed in bfloat16 or wider, within the bound.
A program may use at most 128 MiB of HBM per device.

v0:
```python
import jax
import jax.numpy as jnp
from jax import lax
from jax.sharding import PartitionSpec as P

CAP = 2


def slot_numbers(ab_tiles, slot_tile):
    match = ab_tiles[..., None] == slot_tile
    places = lax.broadcasted_iota(jnp.int32, match.shape, match.ndim - 1)
    return jnp.sum(jnp.where(match, places, 0), axis=-1)


def shards(
    amplitudes, integral_tiles, tile_cd, tile_ab, slot_tile, residual_in, occ_level, vir_level
):
    groups = lax.axis_size("vir")
    mine = lax.axis_index("vir")
    rows = amplitudes.shape[0]
    tile = integral_tiles.shape[-1]
    kind_count = amplitudes.shape[1] // tile
    total_slots = slot_tile.shape[0]
    per_owner = total_slots // groups
    slots_all = slot_numbers(tile_ab, slot_tile)
    every_slot = jnp.arange(total_slots, dtype=jnp.int32)
    reached = jnp.any(slots_all[..., None] == every_slot, axis=1).astype(jnp.int32)
    reached = reached.reshape(groups, groups, per_owner)
    rank = jnp.cumsum(reached, axis=-1) - 1
    picks = jnp.arange(CAP, dtype=jnp.int32)
    hit = (reached[..., None] == 1) & (rank[..., None] == picks)
    within = lax.broadcasted_iota(jnp.int32, hit.shape, 2)
    chosen = jnp.sum(jnp.where(hit, within, 0), axis=2)
    my_kinds = lax.dynamic_index_in_dim(tile_cd, mine, 0, keepdims=False)
    my_slots = lax.dynamic_index_in_dim(slots_all, mine, 0, keepdims=False)
    my_chosen = lax.dynamic_index_in_dim(chosen, mine, 0, keepdims=False)
    owner_of = my_slots // per_owner
    inside = my_slots % per_owner
    candidates = jnp.take(my_chosen, owner_of, axis=0)
    match = candidates == inside[:, None]
    cap_iota = lax.broadcasted_iota(jnp.int32, match.shape, 1)
    column_of = owner_of * CAP + jnp.sum(jnp.where(match, cap_iota, 0), axis=1)
    empty = jnp.zeros((groups * CAP, kind_count, tile, tile), jnp.bfloat16)
    weight = empty.at[column_of, my_kinds].set(
        lax.all_gather(integral_tiles, "occ", axis=1, tiled=True)[0]
    )
    left = amplitudes.reshape(rows, kind_count, tile)
    partial_value = jnp.einsum("rkt,ckts->rcs", left, weight, preferred_element_type=jnp.float32)
    owner_base = jnp.arange(groups, dtype=jnp.int32)[:, None] * per_owner
    places = (owner_base + my_chosen).reshape(-1)
    placing = (places[:, None] == every_slot[None, :]).astype(jnp.float32)
    spread = jnp.einsum("rcs,cq->rqs", partial_value, placing, precision=lax.Precision.HIGHEST)
    summed = lax.psum_scatter(spread, "vir", scatter_dimension=1, tiled=True)
    by_slot = summed.reshape(rows, per_owner * tile)
    return (residual_in + by_slot) / (occ_level[:, None] - vir_level[None, :])


def solution(mesh):
    in_specs = (
        P("occ", "vir"),
        P("vir", "occ", None, None),
        P(),
        P(),
        P(),
        P("occ", "vir"),
        P("occ"),
        P("vir"),
    )
    out_specs = P("occ", "vir")
    return jax.shard_map(shards, mesh=mesh, in_specs=in_specs, out_specs=out_specs, check_vma=False)
```

profile of v0, /device:TPU:1, one launch (start us, length us, event | category | flops | bytes accessed | tf_op | source)
XLA Modules:
  0.0 295.3 jit_solution(15879185883777184707)
XLA Ops:
  6.5 0.0 copy-start
  6.5 0.7 all-gather.2.cloned.1.call-update
  7.3 0.0 reduce-scatter.2.cloned.1.call-start
  7.3 1.1 select_reduce_fusion
  8.4 0.4 fusion.2
  8.8 0.1 copy.35
  8.9 0.1 reduce_window_sum.11
  8.9 0.1 copy.37
  9.0 0.1 copy.36
  9.2 0.1 copy.38
  9.3 0.1 copy.39
  9.4 0.1 squeeze.18
  9.4 0.1 add.112
  9.5 0.1 add.113
  9.7 0.7 gather_fusion
  10.4 0.2 select_reduce_fusion.1
  10.6 0.7 or_select_fusion
  11.4 51.0 %all-gather.2.cloned.1.call-done = bf16[1,256,128,128]{3,2,0,1:T(8,128)(2,1)} async-done(((bf16[1,32,128,128]{3,2,0,1:T(8,128)(2,1)}), bf16[1,256,128,128]{3,2,0,1:T(8,128)(2,1)}) %all-gather.2.cloned.1.call-update) | async-done | bytes 8388624 | tf_op jit(solution)/shard_map/all_gather | solution.py:45
  62.4 8.8 %broadcast_in_dim.40 = bf16[32,24,128,128]{3,2,1,0:T(8,128)(2,1)} broadcast(bf16[]{:T(256)} %constant.68.clone.1), dimensions={} | broadcast | bytes 25165826 | tf_op jit(solution)/shard_map/broadcast_in_dim | solution.py:43
  71.2 39.9 %scatter_fusion = bf16[32,24,128,128]{3,2,1,0:T(8,128)(2,1)} fusion(bf16[32,24,128,128]{3,2,1,0:T(8,128)(2,1)} %broadcast_in_dim.40, s32[256]{0:T(256)S(1)} %bitcast.45, bf16[256,128,128]{2,1,0:T(8,128)(2,1)} %bitcast.46), kind=kCustom, calls=%fused_computation.1 | custom fusion | bytes 25167872 | tf_op jit(solution)/shard_map/scatter | solution.py:44
  111.2 20.1 %convolution_bitcast_fusion.1 = f32[512,32,128]{0,2,1:T(8,128)} fusion(bf16[32,24,128,128]{3,2,1,0:T(8,128)(2,1)} %scatter_fusion, bf16[512,3072]{1,0:T(8,128)(2,1)S(1)} %copy-done), kind=kOutput, calls=%fused_computation.3 | convolution fusion | flops 12884901888 | bytes 36700160 | tf_op jit(solution)/shard_map/rkt,ckts->rcs/dot_general | solution.py:48
  131.2 10.3 %copy.43 = f32[512,32,128]{2,1,0:T(8,128)} copy(f32[512,32,128]{0,2,1:T(8,128)} %convolution_bitcast_fusion.1) | data formatting | bytes 16777216 | tf_op jit(solution)/shard_map/rkt,ckts->rcs/dot_general | solution.py:48
  141.5 9.4 %convolution_bitcast_fusion = f32[512,64,128]{2,1,0:T(8,128)S(1)} fusion(f32[512,32,128]{2,1,0:T(8,128)} %copy.43, s32[32]{0:T(128)S(1)} %add.115), kind=kOutput, calls=%fused_computation.2 | convolution fusion | flops 1610614784 | bytes 25165952 | tf_op jit(solution)/shard_map/rcs,cq->rqs/dot_general | solution.py:52
  150.9 19.5 %copy.44 = f32[512,64,128]{2,0,1:T(8,128)} copy(f32[512,64,128]{2,1,0:T(8,128)S(1)} %convolution_bitcast_fusion) | data formatting | bytes 33554432 | tf_op jit(solution)/shard_map/rcs,cq->rqs/transpose | solution.py:52
  170.4 0.0 reduce-scatter.2.cloned.1.call-update
  170.4 0.0 copy-start.1
  170.5 2.7 copy.46
  173.1 107.4 %reduce-scatter.2.cloned.1.call-done = f32[512,4,128]{2,0,1:T(8,128)} async-done(((f32[512,64,128]{2,0,1:T(8,128)}), f32[512,4,128]{2,0,1:T(8,128)}) %reduce-scatter.2.cloned.1.call-update) | async-done | bytes 1048592 | tf_op jit(solution)/shard_map/reduce_scatter | solution.py:53
  280.5 2.5 copy.45
  283.1 0.0 copy-done.3
  283.1 2.8 fusion.1
  285.9 2.5 copy.47
  (17 shorter events, 0.1 us)
Async XLA Ops:
  6.5 104.6 %copy-start = (bf16[512,3072]{1,0:T(8,128)(2,1)S(1)}, bf16[512,3072]{1,0:T(8,128)(2,1)}, u32[]{:S(2)}) copy-start(bf16[512,3072]{1,0:T(8,128)(2,1)} %param.8) | copy-start | bytes 9437188
  6.5 55.8 %all-gather.2.cloned.1.call-start = ((), (), s32[]{:S(2)}) async-start(), calls=%async_computation.1 | async-start | bytes 9437184 | tf_op jit(solution)/shard_map/all_gather | solution.py:45
  7.3 273.3 %reduce-scatter.2.cloned.1.call-start = ((), (), s32[]{:S(2)}) async-start(), calls=%async_computation.2 | async-start | bytes 17825792 | tf_op jit(solution)/shard_map/reduce_scatter | solution.py:53
  170.4 112.7 %copy-start.2 = (f32[512]{0:T(512)S(1)}, f32[512]{0:T(512)}, u32[]{:S(2)}) copy-start(f32[512]{0:T(512)} %param.15) | copy-start | bytes 6148
  170.4 112.7 %copy-start.3 = (f32[512]{0:T(512)S(1)}, f32[512]{0:T(512)}, u32[]{:S(2)}) copy-start(f32[512]{0:T(512)} %param.14) | copy-start | bytes 6148
  170.4 118.0 %copy-start.1 = (bf16[512,3072]{1,0:T(8,128)(2,1)S(1)}, bf16[512,3072]{1,0:T(8,128)(2,1)}, u32[]{:S(2)}) copy-start(bf16[512,3072]{1,0:T(8,128)(2,1)} %param.8) | copy-start | bytes 9437188
Sparse Core Ops, SparseCore 0:
  9.0 53.2 all-gather.1
  170.6 109.9 reduce-scatter.1
where the time goes:
time: 296 us; the launch traced here: 295 us
  waiting for transfers between devices  159 us (54%)
  local copies, waits for them, and re-layouts  87.7 us (30%)
  matrix products  29.5 us (10%)
  between operations  13.5 us (5%)
  other arithmetic  5.33 us (2%)
    reduce_scatter x1, waiting for transfers between devices, shards(): summed = lax.psum_scatter(spread, 'vir', scatter_dimension=1, tiled=True)  107 us
    all_gather x1, waiting for transfers between devices, shards(): lax.all_gather(integral_tiles, 'occ', axis=1, tiled=True)[0]  51 us
    scatter x1, local copies, waits for them, and re-layouts, shards(): empty.at[column_of, my_kinds]  39.9 us
    dot_general x1, matrix products, shards(): jnp.einsum('rkt,ckts->rcs', left, weight, preferred_element_type=jnp.floa...  20.1 us
    transpose x1, local copies, waits for them, and re-layouts, shards(): jnp.einsum('rcs,cq->rqs', partial_value, placing, precision=lax.Precision...  19.5 us
    dot_general x1, local copies, waits for them, and re-layouts, shards(): jnp.einsum('rkt,ckts->rcs', left, weight, preferred_element_type=jnp.floa...  10.3 us
    dot_general x1, matrix products, shards(): jnp.einsum('rcs,cq->rqs', partial_value, placing, precision=lax.Precision...  9.42 us
    broadcast_in_dim x1, local copies, waits for them, and re-layouts, shards(): empty = jnp.zeros((groups * CAP, kind_count, tile, tile), jnp.bfloat16)  8.84 us
  transfers between devices with their start and end apart: 2, of which 2 were waited for; matrix products, arithmetic and copies ran while one was open for 2% of the time, Pallas kernels for 0%

commit v1 on v0

--- a/solution.py
+++ b/solution.py
@@ -1,9 +1,21 @@
+import functools
 import jax
 import jax.numpy as jnp
 from jax import lax
 from jax.sharding import PartitionSpec as P
+from jax.lax import all_to_all, axis_size
 
 CAP = 2
+
+
+def reach_thing(u_in, across, axis_no):
+    x_new = axis_size(across)
+    mid_arr = jnp.stack([u_in] * x_new, 0)
+    outcome_arr = all_to_all(mid_arr, across, split_axis=0, concat_axis=0)
+    return jnp.concatenate(outcome_arr, axis=axis_no)
+
+
+cut_heads = functools.partial(reach_thing, across="occ", axis_no=1)
 
 
 def slot_numbers(ab_tiles, slot_tile):
@@ -41,9 +53,7 @@
     cap_iota = lax.broadcasted_iota(jnp.int32, match.shape, 1)
     column_of = owner_of * CAP + jnp.sum(jnp.where(match, cap_iota, 0), axis=1)
     empty = jnp.zeros((groups * CAP, kind_count, tile, tile), jnp.bfloat16)
-    weight = empty.at[column_of, my_kinds].set(
-        lax.all_gather(integral_tiles, "occ", axis=1, tiled=True)[0]
-    )
+    weight = empty.at[column_of, my_kinds].set(cut_heads(integral_tiles)[0])
     left = amplitudes.reshape(rows, kind_count, tile)
     partial_value = jnp.einsum("rkt,ckts->rcs", left, weight, preferred_element_type=jnp.float32)
     owner_base = jnp.arange(groups, dtype=jnp.int32)[:, None] * per_owner

time: 296 us -> 349 us (1.18)
  waiting for transfers between devices: 159 us -> 199 us
  local copies, waits for them, and re-layouts: 87.7 us -> 94.5 us
  starting transfers between devices: 0.04 us -> 6.43 us
    all_to_all x0 -> x1, waiting for transfers between devices: none -> 90.6 us  [reach_thing(): outcome_arr = all_to_all(mid_arr, across, split_axis=0, concat_axis=0)]
    all_gather x1 -> x0, waiting for transfers between devices: 51 us -> none  [shards(): lax.all_gather(integral_tiles, 'occ', axis=1, tiled=True)[0]]
    another operation x0 -> x1, local copies, waits for them, and re-layouts: none -> 6.73 us  [reach_thing(): mid_arr = jnp.stack([u_in] * x_new, 0)]
    all_to_all x0 -> x1, starting transfers between devices: none -> 6.43 us  [reach_thing(): outcome_arr = all_to_all(mid_arr, across, split_axis=0, concat_axis=0)]
where the time goes in v1:
time: 349 us; the launch traced here: 348 us
  waiting for transfers between devices  199 us (57%)
  local copies, waits for them, and re-layouts  94.5 us (27%)
  matrix products  29.5 us (8%)
  between operations  13.5 us (4%)
  starting transfers between devices  6.43 us (2%)
  other arithmetic  4.44 us (1%)
    reduce_scatter x1, waiting for transfers between devices, shards(): summed = lax.psum_scatter(spread, 'vir', scatter_dimension=1, tiled=True)  109 us
    all_to_all x1, waiting for transfers between devices, reach_thing(): outcome_arr = all_to_all(mid_arr, across, split_axis=0, concat_axis=0)  90.6 us
    scatter x1, local copies, waits for them, and re-layouts, shards(): weight = empty.at[column_of, my_kinds].set(cut_heads(integral_tiles)[0])  39.9 us
    dot_general x1, matrix products, shards(): jnp.einsum('rkt,ckts->rcs', left, weight, preferred_element_type=jnp.floa...  20.1 us
    transpose x1, local copies, waits for them, and re-layouts, shards(): jnp.einsum('rcs,cq->rqs', partial_value, placing, precision=lax.Precision...  19.5 us
    dot_general x1, local copies, waits for them, and re-layouts, shards(): jnp.einsum('rkt,ckts->rcs', left, weight, preferred_element_type=jnp.floa...  10.3 us
    dot_general x1, matrix products, shards(): jnp.einsum('rcs,cq->rqs', partial_value, placing, precision=lax.Precision...  9.42 us
    broadcast_in_dim x1, local copies, waits for them, and re-layouts, shards(): empty = jnp.zeros((groups * CAP, kind_count, tile, tile), jnp.bfloat16)  8.84 us
  transfers between devices with their start and end apart: 2, of which 2 were waited for; matrix products, arithmetic and copies ran while one was open for 2% of the time, Pallas kernels for 0%

profile of v1, /device:TPU:1, one launch (start us, length us, event | category | flops | bytes accessed | tf_op | source)
XLA Modules:
  0.0 347.8 jit_solution(7738681374906345059)
XLA Ops:
  6.5 0.0 copy-start
  6.5 6.7 %stack.2 = bf16[8,1,32,128,128]{4,3,2,1,0:T(8,128)(2,1)} broadcast(bf16[32,128,128]{2,1,0:T(8,128)(2,1)} %bitcast.46), dimensions={2,3,4} | broadcast | bytes 9437184 | tf_op jit(solution)/shard_map/stack | solution.py:13
  13.3 6.4 %all-to-all-start = ((bf16[8,1,32,128,128]{4,3,2,1,0:T(8,128)(2,1)}), bf16[8,1,32,128,128]{4,3,2,1,0:T(8,128)(2,1)}, u32[]{:S(2)}, u32[]{:S(2)}) async-start(bf16[8,1,32,128,128]{4,3,2,1,0:T(8,128)(2,1)} %stack.2), calls=%async_computation | async-start | bytes 16777216 | tf_op jit(solution)/shard_map/all_to_all | solution.py:14
  19.7 0.0 reduce-scatter.2.cloned.1.call-start
  19.7 0.2 select_reduce_fusion
  19.9 0.4 fusion.2
  20.3 0.1 copy.34
  20.4 0.1 reduce_window_sum.11
  20.5 0.1 copy.36
  20.6 0.1 copy.35
  20.7 0.1 copy.37
  20.8 0.1 copy.38
  20.9 0.1 squeeze.15
  21.0 0.1 add.112
  21.0 0.1 add.113
  21.2 0.7 gather_fusion
  21.9 0.2 select_reduce_fusion.1
  22.2 0.7 or_select_fusion
  22.9 90.6 %all-to-all-done = bf16[8,1,32,128,128]{4,3,2,1,0:T(8,128)(2,1)} async-done(((bf16[8,1,32,128,128]{4,3,2,1,0:T(8,128)(2,1)}), bf16[8,1,32,128,128]{4,3,2,1,0:T(8,128)(2,1)}, u32[]{:S(2)}, u32[]{:S(2)}) %all-to-all-start) | async-done | bytes 8388640 | tf_op jit(solution)/shard_map/all_to_all | solution.py:14
  113.5 8.8 %broadcast_in_dim.40 = bf16[32,24,128,128]{3,2,1,0:T(8,128)(2,1)} broadcast(bf16[]{:T(256)} %constant.68.clone.1), dimensions={} | broadcast | bytes 25165826 | tf_op jit(solution)/shard_map/broadcast_in_dim | solution.py:55
  122.3 39.9 %scatter_fusion = bf16[32,24,128,128]{3,2,1,0:T(8,128)(2,1)} fusion(bf16[32,24,128,128]{3,2,1,0:T(8,128)(2,1)} %broadcast_in_dim.40, s32[256]{0:T(256)S(1)} %bitcast.45, bf16[256,128,128]{2,1,0:T(8,128)(2,1)} %bitcast.10), kind=kCustom, calls=%fused_computation.1 | custom fusion | bytes 25167872 | tf_op jit(solution)/shard_map/scatter | solution.py:56
  162.2 20.1 %convolution_bitcast_fusion.1 = f32[512,32,128]{0,2,1:T(8,128)} fusion(bf16[32,24,128,128]{3,2,1,0:T(8,128)(2,1)} %scatter_fusion, bf16[512,3072]{1,0:T(8,128)(2,1)S(1)} %copy-done), kind=kOutput, calls=%fused_computation.3 | convolution fusion | flops 12884901888 | bytes 36700160 | tf_op jit(solution)/shard_map/rkt,ckts->rcs/dot_general | solution.py:58
  182.3 10.3 %copy.41 = f32[512,32,128]{2,1,0:T(8,128)} copy(f32[512,32,128]{0,2,1:T(8,128)} %convolution_bitcast_fusion.1) | data formatting | bytes 16777216 | tf_op jit(solution)/shard_map/rkt,ckts->rcs/dot_general | solution.py:58
  192.6 9.4 %convolution_bitcast_fusion = f32[512,64,128]{2,1,0:T(8,128)S(1)} fusion(f32[512,32,128]{2,1,0:T(8,128)} %copy.41, s32[32]{0:T(128)S(1)} %add.115), kind=kOutput, calls=%fused_computation.2 | convolution fusion | flops 1610614784 | bytes 25165952 | tf_op jit(solution)/shard_map/rcs,cq->rqs/dot_general | solution.py:62
  202.0 19.5 %copy.42 = f32[512,64,128]{2,0,1:T(8,128)} copy(f32[512,64,128]{2,1,0:T(8,128)S(1)} %convolution_bitcast_fusion) | data formatting | bytes 33554432 | tf_op jit(solution)/shard_map/rcs,cq->rqs/transpose | solution.py:62
  221.6 0.0 reduce-scatter.2.cloned.1.call-update
  221.6 0.0 copy-start.1
  221.6 2.7 copy.44
  224.3 108.8 %reduce-scatter.2.cloned.1.call-done = f32[512,4,128]{2,0,1:T(8,128)} async-done(((f32[512,64,128]{2,0,1:T(8,128)}), f32[512,4,128]{2,0,1:T(8,128)}) %reduce-scatter.2.cloned.1.call-update) | async-done | bytes 1048592 | tf_op jit(solution)/shard_map/reduce_scatter | solution.py:63
  333.1 2.5 copy.43
  335.7 2.8 fusion.1
  338.4 2.5 copy.45
  (21 shorter events, 0.1 us)
Async XLA Ops:
  6.5 155.7 %copy-start = (bf16[512,3072]{1,0:T(8,128)(2,1)S(1)}, bf16[512,3072]{1,0:T(8,128)(2,1)}, u32[]{:S(2)}) copy-start(bf16[512,3072]{1,0:T(8,128)(2,1)} %param.8) | copy-start | bytes 9437188
  13.3 6.4 %copy-start.2 = (s32[16,256]{1,0:T(8,128)S(1)}, s32[16,256]{1,0:T(8,128)}, u32[]{:S(2)}) copy-start(s32[16,256]{1,0:T(8,128)} %param.11) | copy-start | bytes 49156
  13.3 6.4 %copy-start.5 = (s32[64]{0:T(128)S(1)}, s32[64]{0:T(128)}, u32[]{:S(2)}) copy-start(s32[64]{0:T(128)} %param.12) | copy-start | bytes 772
  13.3 100.2 %all-to-all-start = ((bf16[8,1,32,128,128]{4,3,2,1,0:T(8,128)(2,1)}), bf16[8,1,32,128,128]{4,3,2,1,0:T(8,128)(2,1)}, u32[]{:S(2)}, u32[]{:S(2)}) async-start(bf16[8,1,32,128,128]{4,3,2,1,0:T(8,128)(2,1)} %stack.2), calls=%async_computation | async-start | bytes 16777216 | tf_op jit(solution)/shard_map/all_to_all | solution.py:14
  19.7 313.4 %reduce-scatter.2.cloned.1.call-start = ((), (), s32[]{:S(2)}) async-start(), calls=%async_computation.2 | async-start | bytes 17825792 | tf_op jit(solution)/shard_map/reduce_scatter | solution.py:63
  221.6 114.1 %copy-start.3 = (f32[512]{0:T(512)S(1)}, f32[512]{0:T(512)}, u32[]{:S(2)}) copy-start(f32[512]{0:T(512)} %param.15) | copy-start | bytes 6148
  221.6 114.1 %copy-start.4 = (f32[512]{0:T(512)S(1)}, f32[512]{0:T(512)}, u32[]{:S(2)}) copy-start(f32[512]{0:T(512)} %param.14) | copy-start | bytes 6148
  221.6 119.4 %copy-start.1 = (bf16[512,3072]{1,0:T(8,128)(2,1)S(1)}, bf16[512,3072]{1,0:T(8,128)(2,1)}, u32[]{:S(2)}) copy-start(bf16[512,3072]{1,0:T(8,128)(2,1)} %param.8) | copy-start | bytes 9437188
Sparse Core Ops, SparseCore 0:
  221.7 111.3 reduce-scatter.1
